TPU v7x, 128 devices: a whole 4x4x4 slice. The times are simulated.
128 devices in a mesh: pair: 32 (over z, y, x_lo), chol: 4 (over x_hi, core).
Axes of the slice: x: 4 (x_hi: 2, x_lo: 2; x = x_hi * 2 + x_lo), y: 4, z: 4, core: 2. Of those that a mesh axis runs over, the one named last changes fastest.
Arguments:
- left_vectors: bfloat16 [8, 160, 800], P(None, 'pair'), may hold values from -6 to 6
- chol_factors: bfloat16 [160, 800, 2560], P('pair', None, 'chol'), may hold values from -0.046875 to 0.046875
- eps_occ: float32 [160], P('pair'), may hold values from -1.5 to -0.3
- eps_vir: float32 [800], replicated, may hold values from 0.2 to 3
Outputs:
- left_sigma: float32 [8, 160, 800], P(None, 'pair')
All inputs are finite; a program needn't handle non-finite values.
Results may differ from a plain program's by a relative error of at most 0.0016.
Values may be sent and summed in bfloat16 or wider, within the bound.
No kernel may reach another device: no remote copies, remote signals or barrier semaphores. Data moves between devices by JAX's collectives and lax.ppermute only.
A program may use at most 64 MiB of HBM per device.

v0:
```python
import jax
import jax.numpy as jnp
from jax import lax
from jax.sharding import PartitionSpec as P


def body(left_vectors, chol_factors, eps_occ, eps_vir):
    occ_local = chol_factors.shape[0]
    gathered = lax.all_gather(left_vectors, "pair", axis=1, tiled=True)
    coul_part = jnp.einsum(
        "ria,iap->rp", left_vectors, chol_factors, preferred_element_type=jnp.float32
    )
    coul_vec = lax.psum(coul_part, "pair").astype(jnp.bfloat16)
    coulomb = jnp.einsum("iap,rp->ria", chol_factors, coul_vec, preferred_element_type=jnp.float32)
    z_local = jnp.einsum(
        "ibp,rjb->rijp", chol_factors, gathered, preferred_element_type=jnp.float32
    ).astype(jnp.bfloat16)
    exchange_term = jnp.einsum(
        "rijp,jap->ria",
        lax.all_to_all(z_local, "pair", split_axis=2, concat_axis=1, tiled=True),
        chol_factors,
        preferred_element_type=jnp.float32,
    )
    offset = lax.axis_index("pair") * occ_local
    partial_all = -exchange_term
    own_rows = lax.dynamic_slice_in_dim(partial_all, offset, occ_local, 1) + 2.0 * coulomb
    partial_all = lax.dynamic_update_slice_in_dim(partial_all, own_rows, offset, 1)
    summed_all = lax.psum(partial_all, ("pair", "chol"))
    summed = lax.dynamic_slice_in_dim(summed_all, offset, occ_local, 1)
    diagonal_part = (eps_vir[None, None, :] - eps_occ[None, :, None]) * left_vectors.astype(
        jnp.float32
    )
    return diagonal_part + summed


def solution(mesh):
    placed = (P(None, "pair", None), P("pair", None, "chol"), P("pair"), P())
    return jax.shard_map(
        body, mesh=mesh, in_specs=placed, out_specs=P(None, "pair", None), check_vma=False
    )
```

profile of v0, /device:TPU:1, one launch (start us, length us, event | category | flops | bytes accessed | tf_op | source)
XLA Modules:
  0.0 612.2 jit_solution(9357112869376586982)
XLA Ops:
  6.5 0.0 all-gather.2.cloned.1.call-start
  6.5 0.7 all-gather.2.cloned.1.call-update
  7.3 140.7 %all-gather.2.cloned.1.call-done = bf16[8,160,800]{2,0,1:T(8,128)(2,1)} async-done(((bf16[8,5,800]{2,0,1:T(8,128)(2,1)}), bf16[8,160,800]{2,0,1:T(8,128)(2,1)}) %all-gather.2.cloned.1.call-update) | async-done | bytes 2048016 | tf_op jit(solution)/shard_map/all_gather | solution.py:9
  147.9 11.9 %convert_bitcast_fusion = bf16[8,5,160,640]{3,2,1,0:T(8,128)(2,1)S(1)} fusion(bf16[5,800,640]{2,1,0:T(8,128)(2,1)} %param.5, bf16[8,160,800,1]{2,0,1,3:T(8,128)(2,1)} %bitcast.28), kind=kOutput, calls=%fused_computation | convolution fusion | flops 6557696000 | bytes 15360000 | tf_op jit(solution)/shard_map/ibp,rjb->rijp/dot_general | solution.py:15
  159.9 6.1 copy.34
  166.0 0.0 copy-start
  166.0 7.0 %all-to-all-start = ((bf16[8,5,160,640]{3,0,1,2:T(8,128)(2,1)}), bf16[8,5,160,640]{3,0,1,2:T(8,128)(2,1)}, u32[]{:S(2)}, u32[]{:S(2)}) async-start(bf16[8,5,160,640]{3,0,1,2:T(8,128)(2,1)} %copy.34), calls=%async_computation | async-start | bytes 16384000 | tf_op jit(solution)/shard_map/all_to_all | solution.py:20
  173.0 0.0 all-reduce.2.cloned.1.call-start
  173.0 0.0 copy-done
  173.0 0.0 slice-start
  173.1 3.3 convolution_bitcast_fusion
  176.4 206.2 %psum.14 = bf16[8,640]{1,0:T(8,128)(2,1)S(1)} all-reduce(f32[8,640]{1,0:T(8,128)S(1)} %convolution_bitcast_fusion), channel_id=1, replica_groups=mesh['pair'=32,'chol'=4] {'pair'}, use_global_device_ids=true, to_apply=%region_0.0 | all-reduce | flops 5120 | bytes 30720 | tf_op jit(solution)/shard_map/psum | solution.py:13
  382.6 0.0 all-to-all-done
  382.6 0.0 slice-start.1
  382.6 7.3 %copy.36 = bf16[8,32,5,5,640]{4,0,3,2,1:T(8,128)(2,1)} copy(bf16[8,32,5,5,640]{4,0,2,3,1:T(8,128)(2,1)} %bitcast.5) | data formatting | bytes 16384000 | tf_op jit(solution)/shard_map/all_to_all | solution.py:20
  389.9 0.0 slice-done
  390.0 0.0 slice-done.1
  390.0 12.7 %bitcast_negate_fusion = f32[8,160,800]{2,0,1:T(8,128)} fusion(bf16[8,160,5,640]{3,0,2,1:T(8,128)(2,1)} %bitcast.27, bf16[5,800,640]{2,1,0:T(8,128)(2,1)S(1)} %bitcast.26), kind=kOutput, calls=%fused_computation.4 | convolution fusion | flops 6554624000 | bytes 17408000 | tf_op jit(solution)/shard_map/rijp,jap->ria/dot_general | solution.py:18
  402.6 0.0 copy-start.1
  402.6 0.0 copy-start.2
  402.6 3.1 fusion.7
  405.7 0.0 all-reduce.2.cloned.1.call-update
  405.7 0.0 copy-done.1
  405.8 0.0 copy-done.2
  405.8 0.1 broadcast_subtract_fusion
  405.8 198.0 %all-reduce.2.cloned.1.call-done = f32[8,160,800]{2,0,1:T(8,128)} async-done(((f32[8,160,800]{2,0,1:T(8,128)}), f32[8,160,800]{2,0,1:T(8,128)}) %all-reduce.2.cloned.1.call-update) | async-done | bytes 4096016 | tf_op jit(solution)/shard_map/psum | solution.py:28
  603.8 1.6 dynamic-slice_add_fusion
  (1 shorter events, 0.0 us)
Async XLA Ops:
  6.5 141.4 %all-gather.2.cloned.1.call-start = ((), (), s32[]{:S(2)}) async-start(), calls=%async_computation.1 | async-start | bytes 2365440 | tf_op jit(solution)/shard_map/all_gather | solution.py:9
  166.0 7.1 %copy-start = (bf16[8,5,800]{2,0,1:T(8,128)(2,1)S(1)}, bf16[8,5,800]{2,0,1:T(8,128)(2,1)}, u32[]{:S(2)}) copy-start(bf16[8,5,800]{2,0,1:T(8,128)(2,1)} %param.4) | copy-start | bytes 192004
  166.0 216.6 %all-to-all-start = ((bf16[8,5,160,640]{3,0,1,2:T(8,128)(2,1)}), bf16[8,5,160,640]{3,0,1,2:T(8,128)(2,1)}, u32[]{:S(2)}, u32[]{:S(2)}) async-start(bf16[8,5,160,640]{3,0,1,2:T(8,128)(2,1)} %copy.34), calls=%async_computation | async-start | bytes 16384000 | tf_op jit(solution)/shard_map/all_to_all | solution.py:20
  173.0 430.8 %all-reduce.2.cloned.1.call-start = ((), (), s32[]{:S(2)}) async-start(), calls=%async_computation.2 | async-start | bytes 9175040 | tf_op jit(solution)/shard_map/psum | solution.py:28
  173.0 216.9 %slice-start = ((s8[5120000]{0:T(1024)(128)(4,1)}), s8[925696]{0:T(1024)(128)(4,1)S(1)}, s32[]{:S(2)}) async-start(s8[5120000]{0:T(1024)(128)(4,1)} %bitcast.25), calls=%async_computation.3 | async-start | bytes 1851392
  382.6 7.3 %slice-start.1 = ((s8[5120000]{0:T(1024)(128)(4,1)}), s8[4194304]{0:T(1024)(128)(4,1)S(1)}, s32[]{:S(2)}) async-start(s8[5120000]{0:T(1024)(128)(4,1)} %bitcast.25), calls=%async_computation.4 | async-start | bytes 8388608
  402.6 3.1 copy-start.1
  402.6 3.1 copy-start.2
Sparse Core Ops, SparseCore 0:
  9.0 138.8 all-gather.1
  405.9 197.8 all-reduce.1
where the time goes:
time: 612 us
  waiting for transfers between devices  339 us (55%)
  blocking collectives  206 us (34%)
  matrix products  31 us (5%)
  local copies, waits for them, and re-layouts  13.5 us (2%)
  between operations  13.5 us (2%)
  starting transfers between devices  7.04 us (1%)
    psum x1, blocking collectives, body(): coul_vec = lax.psum(coul_part, 'pair').astype(jnp.bfloat16)  206 us
    psum x1, waiting for transfers between devices, body(): summed_all = lax.psum(partial_all, ('pair', 'chol'))  198 us
    all_gather x1, waiting for transfers between devices, body(): gathered = lax.all_gather(left_vectors, 'pair', axis=1, tiled=True)  141 us
    dot_general x1, matrix products, body(): jnp.einsum('rijp,jap->ria', lax.all_to_all(z_local, 'pair', split_axis=2,...  12.7 us
  transfers between devices with their start and end apart: 3, of which 2 were waited for; matrix products, arithmetic and copies ran while one was open for 1% of the time, Pallas kernels for 0%

commit v1 on v0

--- a/solution.py
+++ b/solution.py
@@ -25,7 +25,8 @@
     partial_all = -exchange_term
     own_rows = lax.dynamic_slice_in_dim(partial_all, offset, occ_local, 1) + 2.0 * coulomb
     partial_all = lax.dynamic_update_slice_in_dim(partial_all, own_rows, offset, 1)
-    summed_all = lax.psum(partial_all, ("pair", "chol"))
+    one_axis = lax.psum(partial_all, "chol")
+    summed_all = lax.psum(one_axis, "pair")
     summed = lax.dynamic_slice_in_dim(summed_all, offset, occ_local, 1)
     diagonal_part = (eps_vir[None, None, :] - eps_occ[None, :, None]) * left_vectors.astype(
         jnp.float32

time: 612 us -> 896 us (1.46)
  the two profiles are of different devices: /device:TPU:1 before, /device:TPU:0 now
where the time goes in v1:
time: 896 us
  waiting for transfers between devices  597 us (67%)
  blocking collectives  232 us (26%)
  matrix products  31 us (3%)
  local copies, waits for them, and re-layouts  13.5 us (2%)
  between operations  13.2 us (1%)
    psum x1, waiting for transfers between devices, body(): summed_all = lax.psum(one_axis, 'pair')  341 us
    psum x1, blocking collectives, body(): coul_vec = lax.psum(coul_part, 'pair').astype(jnp.bfloat16)  232 us
    all_gather x1, waiting for transfers between devices, body(): gathered = lax.all_gather(left_vectors, 'pair', axis=1, tiled=True)  160 us
    psum x1, waiting for transfers between devices, body(): one_axis = lax.psum(partial_all, 'chol')  94.9 us
  transfers between devices with their start and end apart: 4, of which 3 were waited for; matrix products, arithmetic and copies ran while one was open for 0% of the time, Pallas kernels for 0%

profile of v1, /device:TPU:0, one launch (start us, length us, event | category | flops | bytes accessed | tf_op | source)
XLA Modules:
  0.0 895.5 jit_solution(1680119577524978352)
XLA Ops:
  6.5 0.0 all-gather.2.cloned.1.call-start
  6.5 0.7 all-gather.2.cloned.1.call-update
  7.3 160.4 %all-gather.2.cloned.1.call-done = bf16[8,160,800]{2,0,1:T(8,128)(2,1)} async-done(((bf16[8,5,800]{2,0,1:T(8,128)(2,1)}), bf16[8,160,800]{2,0,1:T(8,128)(2,1)}) %all-gather.2.cloned.1.call-update) | async-done | bytes 2048016 | tf_op jit(solution)/shard_map/all_gather | solution.py:9
  167.6 11.9 %convert_bitcast_fusion = bf16[8,5,160,640]{3,2,1,0:T(8,128)(2,1)S(1)} fusion(bf16[5,800,640]{2,1,0:T(8,128)(2,1)} %param.5, bf16[8,160,800,1]{2,0,1,3:T(8,128)(2,1)} %bitcast.28), kind=kOutput, calls=%fused_computation | convolution fusion | flops 6557696000 | bytes 15360000 | tf_op jit(solution)/shard_map/ibp,rjb->rijp/dot_general | solution.py:15
  179.6 6.1 copy.34
  185.7 0.0 copy-start
  185.7 7.6 all-to-all-start
  193.3 0.0 all-reduce.3.cloned.1.call-start
  193.3 0.0 copy-done
  193.4 0.0 slice-start
  193.4 3.3 convolution_bitcast_fusion
  196.7 231.7 %psum.21 = bf16[8,640]{1,0:T(8,128)(2,1)S(1)} all-reduce(f32[8,640]{1,0:T(8,128)S(1)} %convolution_bitcast_fusion), channel_id=1, replica_groups=mesh['pair'=32,'chol'=4] {'pair'}, use_global_device_ids=true, to_apply=%region_0.0 | all-reduce | flops 5120 | bytes 30720 | tf_op jit(solution)/shard_map/psum | solution.py:13
  428.4 0.0 all-to-all-done
  428.4 0.0 slice-start.1
  428.4 7.3 copy.36
  435.7 0.0 slice-done
  435.7 0.0 slice-done.1
  435.7 12.7 %bitcast_negate_fusion = f32[8,160,800]{2,0,1:T(8,128)} fusion(bf16[8,160,5,640]{3,0,2,1:T(8,128)(2,1)} %bitcast.27, bf16[5,800,640]{2,1,0:T(8,128)(2,1)S(1)} %bitcast.26), kind=kOutput, calls=%fused_computation.4 | convolution fusion | flops 6554624000 | bytes 17408000 | tf_op jit(solution)/shard_map/rijp,jap->ria/dot_general | solution.py:18
  448.5 3.1 fusion.7
  451.5 0.0 copy-start.1
  451.5 0.0 copy-start.2
  451.5 0.0 all-reduce.3.cloned.1.call-update
  451.6 0.0 all-reduce.5.cloned.1.call-start
  451.6 94.9 %all-reduce.3.cloned.1.call-done = f32[8,160,800]{2,0,1:T(8,128)} async-done(((f32[8,160,800]{2,0,1:T(8,128)}), f32[8,160,800]{2,0,1:T(8,128)}) %all-reduce.3.cloned.1.call-update) | async-done | bytes 4096016 | tf_op jit(solution)/shard_map/psum | solution.py:28
  546.5 0.0 all-reduce.5.cloned.1.call-update
  546.6 0.0 copy-done.1
  546.6 0.0 copy-done.2
  546.6 0.1 broadcast_subtract_fusion
  546.6 340.8 %all-reduce.5.cloned.1.call-done = f32[8,160,800]{2,0,1:T(8,128)} async-done(((f32[8,160,800]{2,0,1:T(8,128)}), f32[8,160,800]{2,0,1:T(8,128)}) %all-reduce.5.cloned.1.call-update) | async-done | bytes 4096016 | tf_op jit(solution)/shard_map/psum | solution.py:29
  887.4 1.6 dynamic-slice_add_fusion
  (1 shorter events, 0.0 us)
Async XLA Ops:
  6.5 161.1 %all-gather.2.cloned.1.call-start = ((), (), s32[]{:S(2)}) async-start(), calls=%async_computation.1 | async-start | bytes 2365440 | tf_op jit(solution)/shard_map/all_gather | solution.py:9
  185.7 7.6 copy-start
  185.7 242.7 %all-to-all-start = ((bf16[8,5,160,640]{3,0,1,2:T(8,128)(2,1)}), bf16[8,5,160,640]{3,0,1,2:T(8,128)(2,1)}, u32[]{:S(2)}, u32[]{:S(2)}) async-start(bf16[8,5,160,640]{3,0,1,2:T(8,128)(2,1)} %copy.34), calls=%async_computation | async-start | bytes 16384000 | tf_op jit(solution)/shard_map/all_to_all | solution.py:20
  193.3 353.2 %all-reduce.3.cloned.1.call-start = ((), (), s32[]{:S(2)}) async-start(), calls=%async_computation.2 | async-start | bytes 9175040 | tf_op jit(solution)/shard_map/psum | solution.py:28
  193.4 242.4 %slice-start = ((s8[5120000]{0:T(1024)(128)(4,1)}), s8[925696]{0:T(1024)(128)(4,1)S(1)}, s32[]{:S(2)}) async-start(s8[5120000]{0:T(1024)(128)(4,1)} %bitcast.25), calls=%async_computation.4 | async-start | bytes 1851392
  428.4 7.3 slice-start.1
  451.5 95.0 %copy-start.1 = (f32[800]{0:T(1024)S(1)}, f32[800]{0:T(1024)}, u32[]{:S(2)}) copy-start(f32[800]{0:T(1024)} %param.7) | copy-start | bytes 9604
  451.5 95.0 %copy-start.2 = (f32[5]{0:T(128)S(1)}, f32[5]{0:T(128)}, u32[]{:S(2)}) copy-start(f32[5]{0:T(128)} %param.6) | copy-start | bytes 64
  451.6 435.9 %all-reduce.5.cloned.1.call-start = ((), (), s32[]{:S(2)}) async-start(), calls=%async_computation.3 | async-start | bytes 9175040 | tf_op jit(solution)/shard_map/psum | solution.py:29
Sparse Core Ops, SparseCore 0:
  9.0 158.6 all-gather.1
  451.7 94.8 all-reduce.2
  549.1 338.3 all-reduce.4
